TPU v7x, 256 devices: a whole 4x4x8 slice. The times are simulated.
256 devices in a mesh: row: 8 (over x, core), col: 32 (over y, z).
Axes of the slice: x: 4, y: 4, z: 8, core: 2. Of those that a mesh axis runs over, the one named last changes fastest.
Arguments:
- upper_panel: float32 [2048, 8192], P('row', 'col')
- lower_panel: float32 [2048, 8192], P('row', 'col')
- pole_values: float32 [2, 8192], P(None, 'col'), may hold values from 0 to 4, as said below
- coupling: float32 [2, 8192], P(None, 'col'), may hold values from -6 to 6
- kept_mask: int32 [2, 8192], P(None, 'col'), may hold values from 0 to 1, as said below
- shifts: float32 [16384], P('col'), may hold values from 0 to 4
- source: int32 [16384], P('col'), may hold values from 0 to 16384, as said below
Outputs:
- vectors: float32 [2, 2048, 16384], P(None, 'row', 'col')
- slab_weight: float32 [16384], P('col')
Inputs may be any that keep to these rules, and one draw needn't show every extreme that they name: source[j] = 16384 marks an undeflated merged column; any other value is the pole whose child column the merged column copies, and no pole is named twice. Each device's 512 merged columns hold from 64 to 384 undeflated columns, and some device holds exactly 384. kept_mask is 0 exactly at the poles named in source. Some device of col holds no deflated pole: every pole of both children that it holds is kept. `pole_values`: every pole lies at least 0.4 / 16384 away from every entry of shifts.
All inputs are finite; a program needn't handle non-finite values.
Results may differ from a plain program's by a relative error of at most 0.0003.
Values sent between devices are 32-bit elements; how exact they have to be, the bound alone decides.
A program may use at most 64 MiB of HBM per device.

v0:
```python
import math
import jax
import jax.numpy as jnp
from jax import lax
from jax.sharding import PartitionSpec as P

N1 = 8192
exact_mode = lax.Precision.HIGHEST


def cauchy_block(pole_vals, weights, shift_vals):
    return weights[:, :, None] / (pole_vals[:, :, None] - shift_vals[None, None, :])


def local(upper_panel, lower_panel, pole_values, coupling, kept_mask, shifts, source):
    rows_here = upper_panel.shape[0]
    own_cols = shifts.shape[0]
    weighted = coupling * kept_mask.astype(jnp.float32)
    undeflated = source == 2 * N1
    child_base = jnp.array([0, N1], jnp.int32)
    zeros_acc = jnp.zeros((rows_here, own_cols), jnp.float32)
    pieces = (
        lax.all_gather(upper_panel, "col", axis=1, tiled=True),
        lax.all_gather(lower_panel, "col", axis=1, tiled=True),
        lax.all_gather(pole_values, "col", axis=1, tiled=True),
        lax.all_gather(weighted, "col", axis=1, tiled=True),
    )
    span_cols = math.gcd(pieces[0].shape[1], 1024)

    def advance(number, running):
        window = [
            lax.dynamic_slice_in_dim(member, number * span_cols, span_cols, 1) for member in pieces
        ]
        first_pole = number * span_cols
        cauchy = cauchy_block(window[2], window[3], shifts)
        indices = first_pole + lax.iota(jnp.int32, span_cols)
        one_hot = indices[None, :, None] + child_base[:, None, None] == source[None, None, :]
        basis_tile = jnp.where(undeflated[None, None, :], cauchy, one_hot.astype(jnp.float32))
        upper_acc = running[0] + jnp.dot(
            window[0], basis_tile[0], precision=exact_mode, preferred_element_type=jnp.float32
        )
        lower_acc = running[1] + jnp.dot(
            window[1], basis_tile[1], precision=exact_mode, preferred_element_type=jnp.float32
        )
        return (upper_acc, lower_acc, running[2] + jnp.sum(cauchy * cauchy, axis=(0, 1)))

    upper_acc, lower_acc, norm_sums = lax.fori_loop(
        0,
        pieces[0].shape[1] // span_cols,
        advance,
        (zeros_acc, zeros_acc, jnp.zeros((own_cols,), jnp.float32)),
    )
    scaling = jnp.where(undeflated, lax.rsqrt(norm_sums), 1.0)
    vectors = jnp.stack([upper_acc * scaling[None, :], lower_acc * scaling[None, :]])
    partial_weight = jnp.sum(vectors * vectors, axis=(0, 1))
    slab_weight = lax.psum(partial_weight, "row") / (2 * rows_here * lax.axis_size("row"))
    return (vectors, slab_weight)


def solution(mesh):
    in_specs = (
        P("row", "col"),
        P("row", "col"),
        P(None, "col"),
        P(None, "col"),
        P(None, "col"),
        P("col"),
        P("col"),
    )
    out_specs = (P(None, "row", "col"), P("col"))
    return jax.shard_map(local, mesh=mesh, in_specs=in_specs, out_specs=out_specs, check_vma=False)
```

profile of v0, /device:TPU:1, one launch (start us, length us, event | category | flops | bytes accessed | tf_op | source)
XLA Modules:
  0.0 310.2 jit_solution(16482954497444541827)
XLA Ops:
  7.2 0.0 all-gather.3.cloned.1.call-start
  7.2 0.7 all-gather.3.cloned.1.call-update
  7.9 0.0 all-gather.5.cloned.1.call-start
  7.9 0.7 all-gather.5.cloned.1.call-update
  8.7 0.7 convert_multiply_fusion
  9.4 41.5 %all_gather.13 = f32[2,8192]{1,0:T(2,128)S(1)} all-gather(f32[2,256]{1,0:T(2,128)S(1)} %convert_multiply_fusion), channel_id=1, replica_groups=mesh['row'=8,'col'=32] {'col'}, dimensions={1}, use_global_device_ids=true | all-gather | bytes 67584 | tf_op jit(solution)/shard_map/all_gather | solution.py:26
  50.9 39.2 %all_gather.14 = f32[2,8192]{1,0:T(2,128)S(1)} all-gather(f32[2,256]{1,0:T(2,128)} %param.12), channel_id=1, replica_groups=mesh['row'=8,'col'=32] {'col'}, dimensions={1}, use_global_device_ids=true | all-gather | bytes 67584 | tf_op jit(solution)/shard_map/all_gather | solution.py:25
  90.1 0.7 broadcast_compare_fusion
  90.8 23.1 %all-gather.3.cloned.1.call-done = f32[256,8192]{1,0:T(8,128)} async-done(((f32[256,256]{1,0:T(8,128)}), f32[256,8192]{1,0:T(8,128)}) %all-gather.3.cloned.1.call-update) | async-done | bytes 8388624 | tf_op jit(solution)/shard_map/all_gather | solution.py:23
  113.9 102.9 %all-gather.5.cloned.1.call-done = f32[256,8192]{1,0:T(8,128)} async-done(((f32[256,256]{1,0:T(8,128)}), f32[256,8192]{1,0:T(8,128)}) %all-gather.5.cloned.1.call-update) | async-done | bytes 8388624 | tf_op jit(solution)/shard_map/all_gather | solution.py:24
  216.8 68.3 %while.18 = (s32[]{:T(128)}, f32[256,512]{1,0:T(8,128)S(1)}, f32[256,512]{1,0:T(8,128)S(1)}, f32[512]{0:T(512)S(1)}, f32[256,8192]{1,0:T(8,128)}, /*index=5*/pre...) while((s32[]{:T(128)}, f32[256,512]{1,0:T(8,128)S(1)}, ...), condition=%wide.region_2.3_spmd.clone, body=%wide.region_0.2_spmd.clone.sunk | while | flops 3229093376 | bytes 12669679 | solution.py:47
  216.9 0.1 broadcast_add_fusion.2
  216.9 1.9 multiply_reduce_fusion.3
  218.8 3.3 %fusion.17 = f32[256,512]{1,0:T(8,128)S(1)} fusion(f32[2,1024,512]{2,1,0:T(8,128)S(1)} %get-tuple-element.347, f32[256,8192]{1,0:T(8,128)} %get-tuple-element.389, s32[]{:T(128)S(6)} %select_n.28, f32[256,512]{1,0:T(8,128)S(1)} %get-tuple-element.366, pred[]{:T(512)S(6)} %compare.3), kind=kOutput, calls=%fused_computation.9.clone.1 | convolution fusion | flops 1610874880 | bytes 4194309 | tf_op jit(solution)/shard_map/while/body/eval_jaxpr/dot_general | solution.py:42
  222.1 3.3 %fusion.16 = f32[256,512]{1,0:T(8,128)S(1)} fusion(f32[2,1024,512]{2,1,0:T(8,128)S(1)} %get-tuple-element.347, f32[256,8192]{1,0:T(8,128)} %get-tuple-element.383, s32[]{:T(128)S(6)} %select_n.28, f32[256,512]{1,0:T(8,128)S(1)} %get-tuple-element.365, pred[]{:T(512)S(6)} %compare.3), kind=kOutput, calls=%fused_computation.8.clone.1 | convolution fusion | flops 1610874880 | bytes 4194309 | tf_op jit(solution)/shard_map/while/body/eval_jaxpr/dot_general | solution.py:39
  225.4 0.1 broadcast_add_fusion.2
  225.5 1.9 multiply_reduce_fusion.3
  227.4 3.3 %fusion.17 = f32[256,512]{1,0:T(8,128)S(1)} fusion(f32[2,1024,512]{2,1,0:T(8,128)S(1)} %get-tuple-element.347, f32[256,8192]{1,0:T(8,128)} %get-tuple-element.389, s32[]{:T(128)S(6)} %select_n.28, f32[256,512]{1,0:T(8,128)S(1)} %get-tuple-element.366, pred[]{:T(512)S(6)} %compare.3), kind=kOutput, calls=%fused_computation.9.clone.1 | convolution fusion | flops 1610874880 | bytes 4194309 | tf_op jit(solution)/shard_map/while/body/eval_jaxpr/dot_general | solution.py:42
  230.6 3.3 %fusion.16 = f32[256,512]{1,0:T(8,128)S(1)} fusion(f32[2,1024,512]{2,1,0:T(8,128)S(1)} %get-tuple-element.347, f32[256,8192]{1,0:T(8,128)} %get-tuple-element.383, s32[]{:T(128)S(6)} %select_n.28, f32[256,512]{1,0:T(8,128)S(1)} %get-tuple-element.365, pred[]{:T(512)S(6)} %compare.3), kind=kOutput, calls=%fused_computation.8.clone.1 | convolution fusion | flops 1610874880 | bytes 4194309 | tf_op jit(solution)/shard_map/while/body/eval_jaxpr/dot_general | solution.py:39
  233.9 0.1 broadcast_add_fusion.2
  234.0 1.9 multiply_reduce_fusion.3
  235.9 3.3 %fusion.17 = f32[256,512]{1,0:T(8,128)S(1)} fusion(f32[2,1024,512]{2,1,0:T(8,128)S(1)} %get-tuple-element.347, f32[256,8192]{1,0:T(8,128)} %get-tuple-element.389, s32[]{:T(128)S(6)} %select_n.28, f32[256,512]{1,0:T(8,128)S(1)} %get-tuple-element.366, pred[]{:T(512)S(6)} %compare.3), kind=kOutput, calls=%fused_computation.9.clone.1 | convolution fusion | flops 1610874880 | bytes 4194309 | tf_op jit(solution)/shard_map/while/body/eval_jaxpr/dot_general | solution.py:42
  239.2 3.3 %fusion.16 = f32[256,512]{1,0:T(8,128)S(1)} fusion(f32[2,1024,512]{2,1,0:T(8,128)S(1)} %get-tuple-element.347, f32[256,8192]{1,0:T(8,128)} %get-tuple-element.383, s32[]{:T(128)S(6)} %select_n.28, f32[256,512]{1,0:T(8,128)S(1)} %get-tuple-element.365, pred[]{:T(512)S(6)} %compare.3), kind=kOutput, calls=%fused_computation.8.clone.1 | convolution fusion | flops 1610874880 | bytes 4194309 | tf_op jit(solution)/shard_map/while/body/eval_jaxpr/dot_general | solution.py:39
  242.5 0.1 broadcast_add_fusion.2
  242.6 1.9 multiply_reduce_fusion.3
  244.5 3.3 %fusion.17 = f32[256,512]{1,0:T(8,128)S(1)} fusion(f32[2,1024,512]{2,1,0:T(8,128)S(1)} %get-tuple-element.347, f32[256,8192]{1,0:T(8,128)} %get-tuple-element.389, s32[]{:T(128)S(6)} %select_n.28, f32[256,512]{1,0:T(8,128)S(1)} %get-tuple-element.366, pred[]{:T(512)S(6)} %compare.3), kind=kOutput, calls=%fused_computation.9.clone.1 | convolution fusion | flops 1610874880 | bytes 4194309 | tf_op jit(solution)/shard_map/while/body/eval_jaxpr/dot_general | solution.py:42
  247.7 3.3 %fusion.16 = f32[256,512]{1,0:T(8,128)S(1)} fusion(f32[2,1024,512]{2,1,0:T(8,128)S(1)} %get-tuple-element.347, f32[256,8192]{1,0:T(8,128)} %get-tuple-element.383, s32[]{:T(128)S(6)} %select_n.28, f32[256,512]{1,0:T(8,128)S(1)} %get-tuple-element.365, pred[]{:T(512)S(6)} %compare.3), kind=kOutput, calls=%fused_computation.8.clone.1 | convolution fusion | flops 1610874880 | bytes 4194309 | tf_op jit(solution)/shard_map/while/body/eval_jaxpr/dot_general | solution.py:39
  251.0 0.1 broadcast_add_fusion.2
  251.1 1.9 multiply_reduce_fusion.3
  253.0 3.3 %fusion.17 = f32[256,512]{1,0:T(8,128)S(1)} fusion(f32[2,1024,512]{2,1,0:T(8,128)S(1)} %get-tuple-element.347, f32[256,8192]{1,0:T(8,128)} %get-tuple-element.389, s32[]{:T(128)S(6)} %select_n.28, f32[256,512]{1,0:T(8,128)S(1)} %get-tuple-element.366, pred[]{:T(512)S(6)} %compare.3), kind=kOutput, calls=%fused_computation.9.clone.1 | convolution fusion | flops 1610874880 | bytes 4194309 | tf_op jit(solution)/shard_map/while/body/eval_jaxpr/dot_general | solution.py:42
  256.3 3.3 %fusion.16 = f32[256,512]{1,0:T(8,128)S(1)} fusion(f32[2,1024,512]{2,1,0:T(8,128)S(1)} %get-tuple-element.347, f32[256,8192]{1,0:T(8,128)} %get-tuple-element.383, s32[]{:T(128)S(6)} %select_n.28, f32[256,512]{1,0:T(8,128)S(1)} %get-tuple-element.365, pred[]{:T(512)S(6)} %compare.3), kind=kOutput, calls=%fused_computation.8.clone.1 | convolution fusion | flops 1610874880 | bytes 4194309 | tf_op jit(solution)/shard_map/while/body/eval_jaxpr/dot_general | solution.py:39
  259.6 0.1 broadcast_add_fusion.2
  259.6 1.9 multiply_reduce_fusion.3
  261.5 3.3 %fusion.17 = f32[256,512]{1,0:T(8,128)S(1)} fusion(f32[2,1024,512]{2,1,0:T(8,128)S(1)} %get-tuple-element.347, f32[256,8192]{1,0:T(8,128)} %get-tuple-element.389, s32[]{:T(128)S(6)} %select_n.28, f32[256,512]{1,0:T(8,128)S(1)} %get-tuple-element.366, pred[]{:T(512)S(6)} %compare.3), kind=kOutput, calls=%fused_computation.9.clone.1 | convolution fusion | flops 1610874880 | bytes 4194309 | tf_op jit(solution)/shard_map/while/body/eval_jaxpr/dot_general | solution.py:42
  264.8 3.3 %fusion.16 = f32[256,512]{1,0:T(8,128)S(1)} fusion(f32[2,1024,512]{2,1,0:T(8,128)S(1)} %get-tuple-element.347, f32[256,8192]{1,0:T(8,128)} %get-tuple-element.383, s32[]{:T(128)S(6)} %select_n.28, f32[256,512]{1,0:T(8,128)S(1)} %get-tuple-element.365, pred[]{:T(512)S(6)} %compare.3), kind=kOutput, calls=%fused_computation.8.clone.1 | convolution fusion | flops 1610874880 | bytes 4194309 | tf_op jit(solution)/shard_map/while/body/eval_jaxpr/dot_general | solution.py:39
  268.1 0.1 broadcast_add_fusion.2
  268.2 1.9 multiply_reduce_fusion.3
  270.1 3.3 %fusion.17 = f32[256,512]{1,0:T(8,128)S(1)} fusion(f32[2,1024,512]{2,1,0:T(8,128)S(1)} %get-tuple-element.347, f32[256,8192]{1,0:T(8,128)} %get-tuple-element.389, s32[]{:T(128)S(6)} %select_n.28, f32[256,512]{1,0:T(8,128)S(1)} %get-tuple-element.366, pred[]{:T(512)S(6)} %compare.3), kind=kOutput, calls=%fused_computation.9.clone.1 | convolution fusion | flops 1610874880 | bytes 4194309 | tf_op jit(solution)/shard_map/while/body/eval_jaxpr/dot_general | solution.py:42
  273.3 3.3 %fusion.16 = f32[256,512]{1,0:T(8,128)S(1)} fusion(f32[2,1024,512]{2,1,0:T(8,128)S(1)} %get-tuple-element.347, f32[256,8192]{1,0:T(8,128)} %get-tuple-element.383, s32[]{:T(128)S(6)} %select_n.28, f32[256,512]{1,0:T(8,128)S(1)} %get-tuple-element.365, pred[]{:T(512)S(6)} %compare.3), kind=kOutput, calls=%fused_computation.8.clone.1 | convolution fusion | flops 1610874880 | bytes 4194309 | tf_op jit(solution)/shard_map/while/body/eval_jaxpr/dot_general | solution.py:39
  276.6 0.1 broadcast_add_fusion.2
  276.7 1.9 multiply_reduce_fusion.3
  278.6 3.3 %fusion.17 = f32[256,512]{1,0:T(8,128)S(1)} fusion(f32[2,1024,512]{2,1,0:T(8,128)S(1)} %get-tuple-element.347, f32[256,8192]{1,0:T(8,128)} %get-tuple-element.389, s32[]{:T(128)S(6)} %select_n.28, f32[256,512]{1,0:T(8,128)S(1)} %get-tuple-element.366, pred[]{:T(512)S(6)} %compare.3), kind=kOutput, calls=%fused_computation.9.clone.1 | convolution fusion | flops 1610874880 | bytes 4194309 | tf_op jit(solution)/shard_map/while/body/eval_jaxpr/dot_general | solution.py:42
  281.9 3.3 %fusion.16 = f32[256,512]{1,0:T(8,128)S(1)} fusion(f32[2,1024,512]{2,1,0:T(8,128)S(1)} %get-tuple-element.347, f32[256,8192]{1,0:T(8,128)} %get-tuple-element.383, s32[]{:T(128)S(6)} %select_n.28, f32[256,512]{1,0:T(8,128)S(1)} %get-tuple-element.365, pred[]{:T(512)S(6)} %compare.3), kind=kOutput, calls=%fused_computation.8.clone.1 | convolution fusion | flops 1610874880 | bytes 4194309 | tf_op jit(solution)/shard_map/while/body/eval_jaxpr/dot_general | solution.py:39
  285.2 0.7 rsqrt_select_fusion
  285.8 0.1 multiply_bitcast_fusion.1
  286.0 1.1 multiply_reduce_fusion.1
  287.1 15.6 %psum.7 = f32[512]{0:T(512)S(1)} all-reduce(f32[512]{0:T(512)S(1)} %get-tuple-element.266), channel_id=1, replica_groups=mesh['row'=8,'col'=32] {'row'}, use_global_device_ids=true, to_apply=%region_4.5 | all-reduce | flops 512 | bytes 4096 | tf_op jit(solution)/shard_map/psum | solution.py:56
  302.7 0.6 broadcast_multiply_fusion
  (35 shorter events, 0.2 us)
Async XLA Ops:
  7.2 106.8 %all-gather.3.cloned.1.call-start = ((), (), s32[]{:S(2)}) async-start(), calls=%async_computation | async-start | bytes 8650752 | tf_op jit(solution)/shard_map/all_gather | solution.py:23
  7.9 209.0 %all-gather.5.cloned.1.call-start = ((), (), s32[]{:S(2)}) async-start(), calls=%async_computation.1 | async-start | bytes 8650752 | tf_op jit(solution)/shard_map/all_gather | solution.py:24
Sparse Core Ops, SparseCore 0:
  10.4 103.4 all-gather.2
  116.4 100.4 all-gather.4
where the time goes:
time: 311 us; the launch traced here: 310 us
  waiting for transfers between devices  127 us (41%)
  blocking collectives  96.3 us (31%)
  matrix products  52.1 us (17%)
  other arithmetic  19.7 us (6%)
  between operations  14.1 us (5%)
    all_gather x1, waiting for transfers between devices, local(): lax.all_gather(lower_panel, 'col', axis=1, tiled=True)  103 us
    all_gather x1, blocking collectives, local(): lax.all_gather(weighted, 'col', axis=1, tiled=True)  41.5 us
    all_gather x1, blocking collectives, local(): lax.all_gather(pole_values, 'col', axis=1, tiled=True)  39.2 us
    dot_general x8, matrix products, advance(): jnp.dot(window[0], basis_tile[0], precision=exact_mode, preferred_element...  26 us
    dot_general x8, matrix products, advance(): jnp.dot(window[1], basis_tile[1], precision=exact_mode, preferred_element...  26 us
    all_gather x1, waiting for transfers between devices, local(): lax.all_gather(upper_panel, 'col', axis=1, tiled=True)  23.1 us
    psum x1, blocking collectives, local(): lax.psum(partial_weight, 'row') / (2 * rows_here * lax.axis_size('row'))  15.6 us
    reduce_sum x8, other arithmetic, advance(): jnp.sum(cauchy * cauchy, axis=(0, 1))  15 us
  transfers between devices with their start and end apart: 2, of which 2 were waited for; matrix products, arithmetic and copies ran while one was open for 0% of the time, Pallas kernels for 0%

commit v1 on v0

--- a/solution.py
+++ b/solution.py
@@ -6,6 +6,14 @@
 
 N1 = 8192
 exact_mode = lax.Precision.HIGHEST
+
+
+def tiled_gather(value, axis, dim):
+    size = lax.axis_size(axis)
+    repeats = [size if d == dim else 1 for d in range(value.ndim)]
+    return lax.all_to_all(
+        jnp.tile(value, repeats), axis, split_axis=dim, concat_axis=dim, tiled=True
+    )
 
 
 def cauchy_block(pole_vals, weights, shift_vals):
@@ -21,7 +29,7 @@
     zeros_acc = jnp.zeros((rows_here, own_cols), jnp.float32)
     pieces = (
         lax.all_gather(upper_panel, "col", axis=1, tiled=True),
-        lax.all_gather(lower_panel, "col", axis=1, tiled=True),
+        tiled_gather(lower_panel, "col", 1),
         lax.all_gather(pole_values, "col", axis=1, tiled=True),
         lax.all_gather(weighted, "col", axis=1, tiled=True),
     )

time: 311 us -> 448 us (1.44)
  blocking collectives: 96.3 us -> 319 us
  waiting for transfers between devices: 127 us -> 0.68 us
  local copies, waits for them, and re-layouts: 0.02 us -> 14.2 us
  starting transfers between devices: 0.08 us -> 12.3 us
  other arithmetic: 19.7 us -> 27.5 us
  matrix products: 52.1 us -> 58.5 us
    all_gather x1, blocking collectives: 41.5 us -> 250 us  [local(): lax.all_gather(weighted, 'col', axis=1, tiled=True)]
    all_gather x1 -> x0, waiting for transfers between devices: 103 us -> none  [local(): lax.all_gather(lower_panel, 'col', axis=1, tiled=True)]
    all_gather x1, waiting for transfers between devices: 23.1 us -> 0.01 us  [local(): lax.all_gather(upper_panel, 'col', axis=1, tiled=True)]
    psum x1, blocking collectives: 15.6 us -> 32.6 us  [local(): lax.psum(partial_weight, 'row') / (2 * rows_here * lax.axis_size('row'))]
    all_to_all x0 -> x1, starting transfers between devices: none -> 12.3 us  [tiled_gather(): lax.all_to_all(jnp.tile(value, repeats), axis, split_axis=dim, concat_axi...]
    reduce_sum x8, other arithmetic: 15 us -> 24.9 us  [advance(): jnp.sum(cauchy * cauchy, axis=(0, 1))]
    all_to_all x0 -> x1, local copies, waits for them, and re-layouts: none -> 8.94 us  [tiled_gather(): lax.all_to_all(jnp.tile(value, repeats), axis, split_axis=dim, concat_axi...]
    dot_general x8, matrix products: 26 us -> 32.5 us  [advance(): jnp.dot(window[1], basis_tile[1], precision=exact_mode, preferred_element...]
  transfers between devices with their start and end apart: 2 -> 2, of which waited for: 2 -> 0; matrix products, arithmetic and copies ran while one was open for 0% -> 2% of each run, Pallas kernels for 0% -> 0%
where the time goes in v1:
time: 448 us; the launch traced here: 447 us
  blocking collectives  319 us (71%)
  matrix products  58.5 us (13%)
  other arithmetic  27.5 us (6%)
  local copies, waits for them, and re-layouts  14.2 us (3%)
  between operations  14.1 us (3%)
  starting transfers between devices  12.3 us (3%)
    all_gather x1, blocking collectives, local(): lax.all_gather(weighted, 'col', axis=1, tiled=True)  250 us
    all_gather x1, blocking collectives, local(): lax.all_gather(pole_values, 'col', axis=1, tiled=True)  36.8 us
    psum x1, blocking collectives, local(): lax.psum(partial_weight, 'row') / (2 * rows_here * lax.axis_size('row'))  32.6 us
    dot_general x8, matrix products, advance(): jnp.dot(window[1], basis_tile[1], precision=exact_mode, preferred_element...  32.5 us
    dot_general x8, matrix products, advance(): jnp.dot(window[0], basis_tile[0], precision=exact_mode, preferred_element...  26 us
    reduce_sum x8, other arithmetic, advance(): jnp.sum(cauchy * cauchy, axis=(0, 1))  24.9 us
    all_to_all x1, starting transfers between devices, tiled_gather(): lax.all_to_all(jnp.tile(value, repeats), axis, split_axis=dim, concat_axi...  12.3 us
  transfers between devices with their start and end apart: 2, of which 0 were waited for; matrix products, arithmetic and copies ran while one was open for 2% of the time, Pallas kernels for 0%

profile of v1, /device:TPU:1, one launch (start us, length us, event | category | flops | bytes accessed | tf_op | source)
XLA Modules:
  0.0 446.9 jit_solution(11360790811784381918)
XLA Ops:
  7.2 5.1 %tile.2 = f32[256,32,256]{2,0,1:T(8,128)} broadcast(f32[256,256]{1,0:T(8,128)} %param.11), dimensions={0,2} | broadcast | bytes 8650752 | tf_op jit(solution)/shard_map/tile | solution.py:15
  12.3 12.3 %all-to-all-start = ((f32[256,32,256]{2,0,1:T(8,128)}), f32[256,32,256]{2,0,1:T(8,128)}, u32[]{:S(2)}, u32[]{:S(2)}) async-start(f32[256,32,256]{2,0,1:T(8,128)} %tile.2), calls=%async_computation | async-start | bytes 16777216 | tf_op jit(solution)/shard_map/all_to_all | solution.py:14
  24.6 0.0 all-gather.2.cloned.1.call-start
  24.6 0.7 all-gather.2.cloned.1.call-update
  25.4 0.0 copy-done.3
  25.4 0.0 copy-done.4
  25.4 249.6 %all_gather.10 = f32[2,8192]{1,0:T(2,128)S(1)} all-gather(f32[2,256]{1,0:T(2,128)S(1)} %convert_multiply_fusion), channel_id=1, replica_groups=mesh['row'=8,'col'=32] {'col'}, dimensions={1}, use_global_device_ids=true | all-gather | bytes 67584 | tf_op jit(solution)/shard_map/all_gather | solution.py:34
  275.0 36.8 %all_gather.11 = f32[2,8192]{1,0:T(2,128)S(1)} all-gather(f32[2,256]{1,0:T(2,128)S(1)} %copy-done.5), channel_id=1, replica_groups=mesh['row'=8,'col'=32] {'col'}, dimensions={1}, use_global_device_ids=true | all-gather | bytes 67584 | tf_op jit(solution)/shard_map/all_gather | solution.py:33
  311.9 0.0 copy-start.2
  311.9 0.0 all-to-all-done
  311.9 8.9 %copy.12 = f32[256,32,256]{0,2,1:T(8,128)} copy(f32[256,32,256]{2,0,1:T(8,128)} %all-to-all-done) | data formatting | bytes 16777216 | tf_op jit(solution)/shard_map/all_to_all | solution.py:14
  320.8 84.8 %while.18 = (s32[]{:T(128)}, f32[256,512]{1,0:T(8,128)S(1)}, f32[256,512]{1,0:T(8,128)S(1)}, f32[512]{0:T(512)S(1)}, f32[256,8192]{1,0:T(8,128)}, /*index=5*/pre...) while((s32[]{:T(128)}, f32[256,512]{1,0:T(8,128)S(1)}, ...), condition=%wide.region_2.3_spmd.clone, body=%wide.region_0.2_spmd.clone.sunk | while | flops 3229093376 | bytes 29446912 | solution.py:55
  320.9 0.1 broadcast_add_fusion.2
  320.9 3.1 multiply_reduce_fusion.3
  324.0 4.1 fusion.17
  328.1 3.3 fusion.16
  331.5 0.1 broadcast_add_fusion.2
  331.5 3.1 multiply_reduce_fusion.3
  334.6 4.1 fusion.17
  338.7 3.3 fusion.16
  342.1 0.1 broadcast_add_fusion.2
  342.1 3.1 multiply_reduce_fusion.3
  345.3 4.1 fusion.17
  349.3 3.3 fusion.16
  352.7 0.1 broadcast_add_fusion.2
  352.7 3.1 multiply_reduce_fusion.3
  355.9 4.1 fusion.17
  359.9 3.3 fusion.16
  363.3 0.1 broadcast_add_fusion.2
  363.3 3.1 multiply_reduce_fusion.3
  366.5 4.1 fusion.17
  370.5 3.3 fusion.16
  373.9 0.1 broadcast_add_fusion.2
  373.9 3.1 multiply_reduce_fusion.3
  377.1 4.1 fusion.17
  381.1 3.3 fusion.16
  384.5 0.1 broadcast_add_fusion.2
  384.5 3.1 multiply_reduce_fusion.3
  387.7 4.1 fusion.17
  391.7 3.3 fusion.16
  395.1 0.1 broadcast_add_fusion.2
  395.1 3.1 multiply_reduce_fusion.3
  398.3 4.1 fusion.17
  402.3 3.3 fusion.16
  405.6 0.1 multiply_bitcast_fusion.1
  405.8 1.1 multiply_reduce_fusion.1
  406.9 32.6 %psum.7 = f32[512]{0:T(512)S(1)} all-reduce(f32[512]{0:T(512)S(1)} %get-tuple-element.288), channel_id=1, replica_groups=mesh['row'=8,'col'=32] {'row'}, use_global_device_ids=true, to_apply=%region_4.5 | all-reduce | flops 512 | bytes 4096 | tf_op jit(solution)/shard_map/psum | solution.py:64
  439.5 0.6 broadcast_multiply_fusion
  (62 shorter events, 0.3 us)
Async XLA Ops:
  12.3 13.1 %copy-start.3 = (f32[2,256]{1,0:T(2,128)S(1)}, f32[2,256]{1,0:T(2,128)}, u32[]{:S(2)}) copy-start(f32[2,256]{1,0:T(2,128)} %param.13) | copy-start | bytes 6148
  12.3 13.1 %copy-start.4 = (s32[2,256]{1,0:T(2,128)S(1)}, s32[2,256]{1,0:T(2,128)}, u32[]{:S(2)}) copy-start(s32[2,256]{1,0:T(2,128)} %param.14) | copy-start | bytes 6148
  12.3 262.8 %copy-start.5 = (f32[2,256]{1,0:T(2,128)S(1)}, f32[2,256]{1,0:T(2,128)}, u32[]{:S(2)}) copy-start(f32[2,256]{1,0:T(2,128)} %param.12) | copy-start | bytes 6148
  12.3 299.6 %copy-start.1 = (s32[512]{0:T(512)S(1)}, s32[512]{0:T(512)}, u32[]{:S(2)}) copy-start(s32[512]{0:T(512)} %param.16) | copy-start | bytes 6148
  12.3 299.6 %all-to-all-start = ((f32[256,32,256]{2,0,1:T(8,128)}), f32[256,32,256]{2,0,1:T(8,128)}, u32[]{:S(2)}, u32[]{:S(2)}) async-start(f32[256,32,256]{2,0,1:T(8,128)} %tile.2), calls=%async_computation | async-start | bytes 16777216 | tf_op jit(solution)/shard_map/all_to_all | solution.py:14
  24.6 296.2 %all-gather.2.cloned.1.call-start = ((), (), s32[]{:S(2)}) async-start(), calls=%async_computation.1 | async-start | bytes 8650752 | tf_op jit(solution)/shard_map/all_gather | solution.py:31
  311.9 9.0 %copy-start.2 = (f32[512]{0:T(512)S(1)}, f32[512]{0:T(512)}, u32[]{:S(2)}) copy-start(f32[512]{0:T(512)} %param.15) | copy-start | bytes 6148
  324.0 4.1 copy-start
  334.6 4.1 copy-start
  345.2 4.1 copy-start
  355.9 4.1 copy-start
  366.5 4.1 copy-start
  377.1 4.1 copy-start
  387.7 4.1 copy-start
  398.3 4.1 copy-start
Sparse Core Ops, SparseCore 0:
  27.9 237.8 all-gather.1
